TPU v7x, 32 devices: a whole 2x2x4 slice. The times are simulated.
32 devices in a mesh: fsdp: 4 (over y, x), rep: 8 (over z, core).
Axes of the slice: x: 2, y: 2, z: 4, core: 2. Of those that a mesh axis runs over, the one named last changes fastest.
Arguments:
- tokens: bfloat16 [64, 256, 384], P(('fsdp', 'rep')), may hold values from -6 to 6
- conditions: bfloat16 [64, 384], P(('fsdp', 'rep')), may hold values from -6 to 6
- assignment: int32 [64], P(('fsdp', 'rep')), may hold values from 0 to 63, each once
- params: float32 [2654208], P('fsdp')
- momentum: float32 [2654208], P('fsdp'), may hold values from -24 to 24
- cotangent: bfloat16 [64, 256, 384], P(('fsdp', 'rep')), may hold values from -6 to 6
Outputs:
- blended: bfloat16 [64, 256, 384], P(('fsdp', 'rep'))
- grad_tokens: float32 [64, 256, 384], P(('fsdp', 'rep'))
- grad_params: float32 [2654208], P('fsdp')
- new_params: float32 [2654208], P('fsdp')
- new_momentum: float32 [2654208], P('fsdp')
Inputs may be any that keep to these rules, and one draw needn't show every extreme that they name: assignment is a permutation of the latent numbers.
All inputs are finite; a program needn't handle non-finite values.
Results may differ from a plain program's by a relative error of at most 0.014.
The roundings to bfloat16 on the way count: a program that leaves them out, or rounds other values in their place, can miss the bound.
Values may be sent and summed in bfloat16 or wider, within the bound.
No kernel may reach another device: no remote copies, remote signals or barrier semaphores. Data moves between devices by JAX's collectives and lax.ppermute only.
A program may use at most 192 MiB of HBM per device.

v0:
```python
import math
import jax
import jax.numpy as jnp
from jax import lax
from jax.sharding import PartitionSpec as P

D = 384
HEADS = 6
HD = 64
FF = 1536
SEQ = 256
NS_ITERS = 3
LN_EPSILON = 1e-06
MOMENTUM_RATE = 0.95
LEARN_RATE = 0.2
COEFF_A = 3.4445
COEFF_B = -4.775
COEFF_C = 2.0315


def matrix_shapes():
    return [(D, 6 * D), (D, 3 * D), (D, D), (D, FF), (FF, D)]


def unpack(flat_vec):
    pieces = []
    offset = 0
    for rows_count, cols_count in matrix_shapes():
        pieces.append(
            flat_vec[offset : offset + rows_count * cols_count].reshape(rows_count, cols_count)
        )
        offset += rows_count * cols_count
    return pieces


def matmul(lhs_array, rhs_array):
    return jnp.dot(lhs_array, rhs_array, preferred_element_type=jnp.float32)


def contract(pattern, lhs_array, rhs_array):
    return jnp.einsum(pattern, lhs_array, rhs_array, preferred_element_type=jnp.float32)


def modulate(hidden, shifts, scales):
    center = jnp.mean(hidden, axis=-1, keepdims=True)
    spread = jnp.mean(jnp.square(hidden - center), axis=-1, keepdims=True)
    return (hidden - center) * lax.rsqrt(spread + LN_EPSILON) * (1.0 + scales) + shifts


def gelu_tanh(values_in):
    return jax.nn.gelu(values_in, approximate=True)


def orthogonalize(matrix):
    flipped = matrix.shape[0] > matrix.shape[1]
    current = matrix.T if flipped else matrix
    current = current / (jnp.sqrt(jnp.sum(current * current)) + 1e-07)
    for newton_step in range(NS_ITERS):
        square = jnp.dot(current, current.T, precision=lax.Precision.HIGHEST)
        polynomial = COEFF_B * square + COEFF_C * jnp.dot(
            square, square, precision=lax.Precision.HIGHEST
        )
        current = COEFF_A * current + jnp.dot(polynomial, current, precision=lax.Precision.HIGHEST)
    return current.T if flipped else current


def update_scale(rows_count, cols_count):
    return LEARN_RATE * 0.2 * math.sqrt(max(rows_count, cols_count))


def scaled_update(matrix, factor):
    return (factor * orthogonalize(matrix)).reshape(-1)


def empty_update(matrix, factor):
    return jnp.zeros((matrix.shape[0] * matrix.shape[1],), jnp.float32)


def forward_pass(tokens, cond_rows, weights):
    adaln_weight, qkv_weight, out_weight, up_weight, down_weight = weights
    batch_size = tokens.shape[0]
    row_count = batch_size * SEQ
    silu_cond = jax.nn.silu(cond_rows.astype(jnp.float32)).astype(jnp.bfloat16)
    modulation = matmul(silu_cond, adaln_weight).reshape(batch_size, 6, 1, D)
    mod_parts = tuple((modulation[:, position] for position in range(6)))
    shift_attn, scale_attn, gate_attn, shift_mlp, scale_mlp, gate_mlp = mod_parts
    residual = tokens.astype(jnp.float32)
    attn_input = modulate(residual, shift_attn, scale_attn).astype(jnp.bfloat16)
    qkv_all = matmul(attn_input.reshape(row_count, D), qkv_weight).astype(jnp.bfloat16)
    qkv_heads = qkv_all.reshape(batch_size, SEQ, 3, HEADS, HD).transpose(2, 0, 3, 1, 4)
    queries, key_vecs, value_vecs = (qkv_heads[0], qkv_heads[1], qkv_heads[2])
    scores = contract("bhqd,bhkd->bhqk", queries, key_vecs) * HD ** (-0.5)
    log_total = jax.nn.logsumexp(scores, axis=-1, keepdims=True)
    attn_probs = jnp.exp(scores - log_total).astype(jnp.bfloat16)
    attn_mixed = contract("bhqk,bhkd->bhqd", attn_probs, value_vecs).astype(jnp.bfloat16)
    attn_mixed = attn_mixed.transpose(0, 2, 1, 3).reshape(row_count, D)
    attn_out = matmul(attn_mixed, out_weight).reshape(batch_size, SEQ, D)
    after_attn = residual + gate_attn * attn_out
    mlp_input = (
        modulate(after_attn, shift_mlp, scale_mlp).astype(jnp.bfloat16).reshape(row_count, D)
    )
    pre_act = matmul(mlp_input, up_weight)
    activated = gelu_tanh(pre_act).astype(jnp.bfloat16)
    mlp_out = matmul(activated, down_weight).reshape(batch_size, SEQ, D)
    blended = (after_attn + gate_mlp * mlp_out).astype(jnp.bfloat16)
    kept_state = (
        silu_cond,
        mod_parts,
        residual,
        attn_input,
        queries,
        key_vecs,
        value_vecs,
        log_total,
        attn_mixed,
        attn_out,
        after_attn,
        mlp_input,
        pre_act,
        activated,
        mlp_out,
    )
    return (blended, kept_state)


def backward_pass(kept_state, weights, cotangent):
    (
        silu_cond,
        mod_parts,
        residual,
        attn_input,
        queries,
        key_vecs,
        value_vecs,
        log_total,
        attn_mixed,
        attn_out,
        after_attn,
        mlp_input,
        pre_act,
        activated,
        mlp_out,
    ) = kept_state
    adaln_weight, qkv_weight, out_weight, up_weight, down_weight = weights
    shift_attn, scale_attn, gate_attn, shift_mlp, scale_mlp, gate_mlp = mod_parts
    batch_size = cotangent.shape[0]
    row_count = batch_size * SEQ
    upstream = cotangent.astype(jnp.float32)
    grad_gate_mlp = jnp.sum(upstream * mlp_out, axis=1, keepdims=True)
    grad_mlp_out = (upstream * gate_mlp).astype(jnp.bfloat16).reshape(row_count, D)
    grad_down = matmul(activated.T, grad_mlp_out)
    grad_act = matmul(grad_mlp_out, down_weight.T)
    grad_pre = jax.vjp(gelu_tanh, pre_act)[1](grad_act)[0].astype(jnp.bfloat16)
    grad_up = matmul(mlp_input.T, grad_pre)
    grad_mlp_in = matmul(grad_pre, up_weight.T).reshape(batch_size, SEQ, D)
    grad_after, grad_shift_mlp, grad_scale_mlp = jax.vjp(
        modulate, after_attn, shift_mlp, scale_mlp
    )[1](grad_mlp_in)
    grad_after = upstream + grad_after
    grad_gate_attn = jnp.sum(grad_after * attn_out, axis=1, keepdims=True)
    grad_attn_out = (grad_after * gate_attn).astype(jnp.bfloat16).reshape(row_count, D)
    grad_outw = matmul(attn_mixed.T, grad_attn_out)
    grad_mixed = matmul(grad_attn_out, out_weight.T).astype(jnp.bfloat16)
    grad_mixed = grad_mixed.reshape(batch_size, SEQ, HEADS, HD).transpose(0, 2, 1, 3)
    scores = contract("bhqd,bhkd->bhqk", queries, key_vecs) * HD ** (-0.5)
    probs_full = jnp.exp(scores - log_total)
    grad_values = contract("bhqk,bhqd->bhkd", probs_full.astype(jnp.bfloat16), grad_mixed)
    grad_probs = contract("bhqd,bhkd->bhqk", grad_mixed, value_vecs)
    row_dots = jnp.sum(probs_full * grad_probs, axis=-1, keepdims=True)
    grad_scores = (probs_full * (grad_probs - row_dots) * HD ** (-0.5)).astype(jnp.bfloat16)
    grad_queries = contract("bhqk,bhkd->bhqd", grad_scores, key_vecs)
    grad_keys = contract("bhqk,bhqd->bhkd", grad_scores, queries)
    grad_qkv = jnp.stack([grad_queries, grad_keys, grad_values], axis=0).transpose(1, 3, 0, 2, 4)
    grad_qkv = grad_qkv.reshape(row_count, 3 * D).astype(jnp.bfloat16)
    grad_qkvw = matmul(attn_input.reshape(row_count, D).T, grad_qkv)
    grad_attn_in = matmul(grad_qkv, qkv_weight.T).reshape(batch_size, SEQ, D)
    grad_resid, grad_shift_attn, grad_scale_attn = jax.vjp(
        modulate, residual, shift_attn, scale_attn
    )[1](grad_attn_in)
    grad_tokens = grad_after + grad_resid
    grad_mod = jnp.concatenate(
        [
            grad_shift_attn,
            grad_scale_attn,
            grad_gate_attn,
            grad_shift_mlp,
            grad_scale_mlp,
            grad_gate_mlp,
        ],
        axis=1,
    )
    grad_mod = grad_mod.reshape(batch_size, 6 * D).astype(jnp.bfloat16)
    grad_adaln = matmul(silu_cond.T, grad_mod)
    flat_grads = jnp.concatenate(
        [
            grad_adaln.reshape(-1),
            grad_qkvw.reshape(-1),
            grad_outw.reshape(-1),
            grad_up.reshape(-1),
            grad_down.reshape(-1),
        ]
    )
    return (grad_tokens, flat_grads)


def on_device(tokens, conditions, assignment, params, momentum, cotangent):
    cond_table = lax.all_gather(conditions, ("fsdp", "rep"), axis=0, tiled=True)
    cond_rows = jnp.take(cond_table, assignment, axis=0)
    low_params = params.astype(jnp.bfloat16)
    gathered = lax.all_gather(low_params, "fsdp", axis=0, tiled=True)
    blended, kept_state = forward_pass(tokens, cond_rows, unpack(gathered))
    back_flat = lax.all_gather(low_params, "fsdp", axis=0, tiled=True)
    grad_tokens, flat_grads = backward_pass(kept_state, unpack(back_flat), cotangent)
    group_part = lax.psum_scatter(flat_grads, "fsdp", scatter_dimension=0, tiled=True)
    full_grad = lax.psum(group_part, "rep")
    new_momentum = MOMENTUM_RATE * momentum + full_grad
    whole_mom = lax.all_gather(new_momentum, "fsdp", axis=0, tiled=True)
    fsdp_rank = lax.axis_index("fsdp")
    group_size = lax.axis_size("fsdp")
    shard_len = params.shape[0]
    updates = []
    offset = 0
    for rows_count, cols_count in matrix_shapes():
        length = rows_count * cols_count
        piece = whole_mom[offset : offset + length].reshape(rows_count, cols_count)
        factor = jnp.float32(update_scale(rows_count, cols_count))
        owner_rank = (offset // shard_len + group_size // 2) % group_size
        updates.append(
            lax.cond(fsdp_rank == owner_rank, scaled_update, empty_update, piece, factor)
        )
        offset += length
    local_update = lax.psum_scatter(
        jnp.concatenate(updates), "fsdp", scatter_dimension=0, tiled=True
    )
    new_params = params - local_update
    return (blended, grad_tokens, full_grad, new_params, new_momentum)


def solution(mesh):
    in_specs = (
        P(("fsdp", "rep"), None, None),
        P(("fsdp", "rep"), None),
        P(("fsdp", "rep")),
        P("fsdp"),
        P("fsdp"),
        P(("fsdp", "rep"), None, None),
    )
    out_specs = (
        P(("fsdp", "rep"), None, None),
        P(("fsdp", "rep"), None, None),
        P("fsdp"),
        P("fsdp"),
        P("fsdp"),
    )
    return jax.shard_map(
        on_device, mesh=mesh, in_specs=in_specs, out_specs=out_specs, check_vma=False
    )
```

profile of v0, /device:TPU:0, one launch (start us, length us, event | category | flops | bytes accessed | tf_op | source)
XLA Modules:
  0.0 911.6 jit_solution(14796318998570174122)
XLA Ops:
  7.2 3.0 convert_element_type.90
  10.3 44.1 %all-gather = bf16[32,2,384]{2,1,0:T(2,128)(2,1)S(1)} all-gather(bf16[1,2,384]{2,1,0:T(2,128)(2,1)S(1)} %bitcast.245), channel_id=1, replica_groups=mesh['fsdp'=4,'rep'=8] {'fsdp','rep'}, dimensions={0}, use_global_device_ids=true | all-gather | bytes 50688 | tf_op jit(solution)/shard_map/all_gather | solution.py:207
  55.5 19.7 %all-gather.4.cloned.1.call-done = bf16[2654208]{0:T(1024)(128)(2,1)} async-done(((bf16[663552]{0:T(1024)(128)(2,1)}), bf16[2654208]{0:T(1024)(128)(2,1)}) %all-gather.4.cloned.1.call-update) | async-done | bytes 5308432 | tf_op jit(solution)/shard_map/all_gather | solution.py:210
  79.1 2.0 reshape.358
  81.1 2.0 slice.162
  88.2 2.2 reshape.357
  90.4 2.2 slice.172
  92.5 3.0 slice.157
  95.5 2.8 copy.42
  99.5 2.1 fusion.67
  108.5 2.8 fusion.36
  111.2 2.2 fusion.116
  115.5 2.4 fusion.117
  118.0 2.5 fusion.72
  123.3 1.9 copy.47
  127.1 2.5 convolution_bitcast_fusion
  129.6 3.3 fusion.73
  132.9 5.2 fusion.49
  138.1 5.1 fusion.52
  144.6 2.3 copy.55
  153.1 3.4 reshape.341
  158.1 2.5 fusion.68
  164.9 2.1 reshape.337
  167.0 4.1 constant_dynamic-update-slice_fusion.6
  179.8 205.9 %all-reduce.8.cloned.1.call-done = f32[2654208]{0:T(1024)} async-done(((f32[2654208]{0:T(1024)}), f32[2654208]{0:T(1024)}) %all-reduce.8.cloned.1.call-update) | async-done | bytes 10616848
  385.8 3.4 dynamic-slice.1
  389.3 69.3 %all-reduce.6.cloned.1.call-done = f32[663552]{0:T(1024)} async-done(((f32[663552]{0:T(1024)}), f32[663552]{0:T(1024)}) %all-reduce.6.cloned.1.call-update) | async-done | bytes 2654224 | tf_op jit(solution)/shard_map/psum | solution.py:215
  458.5 3.6 multiply_add_fusion.3
  462.2 105.5 %all-gather.6.cloned.1.call-done = f32[2654208]{0:T(1024)} async-done(((f32[663552]{0:T(1024)}), f32[2654208]{0:T(1024)}) %all-gather.6.cloned.1.call-update) | async-done | bytes 10616848 | tf_op jit(solution)/shard_map/all_gather | solution.py:217
  567.7 9.3 %conditional.5 = (f32[884736]{0:T(1024)S(1)}) conditional(s32[]{:T(128)} %convert_element_type.110, () %tuple.38, f32[2654208]{0:T(1024)} %all-gather.6.cloned.1.call-done), branch_computations={%region_21.22_spmd, %region_22.24_spmd} | conditional | flops 26509787136 | bytes 63701028 | solution.py:229
  577.0 2.1 constant_dynamic-update-slice_fusion.7
  579.1 14.8 %conditional.6 = (f32[442368]{0:T(1024)S(1)}) conditional(s32[]{:T(128)} %convert_element_type.111, () %tuple.39, f32[2654208]{0:T(1024)} %all-gather.6.cloned.1.call-done), branch_computations={%region_24.25_spmd, %region_25.27_spmd} | conditional | flops 14274772992 | bytes 35389476 | solution.py:229
  595.3 15.7 %conditional.7 = (f32[147456]{0:T(1024)S(1)}) conditional(s32[]{:T(128)} %convert_element_type.112, () %tuple.40, f32[2654208]{0:T(1024)} %all-gather.6.cloned.1.call-done), branch_computations={%region_27.28_spmd, %region_28.30_spmd} | conditional | flops 6118096896 | bytes 16515108 | solution.py:229
  611.8 41.5 %conditional.8 = (f32[589824]{0:T(1024)S(1)}) conditional(s32[]{:T(128)} %convert_element_type.112, () %tuple.41, f32[2654208]{0:T(1024)} %all-gather.6.cloned.1.call-done), branch_computations={%region_30.31_spmd, %region_31.33_spmd} | conditional | flops 18353111040 | bytes 44826660 | solution.py:229
  611.8 2.9 multiply_reduce_fusion.3
  615.4 3.2 slice_divide_fusion.3
  618.6 2.4 div.75
  621.1 4.0 fusion.109
  626.3 4.0 convolution_add_fusion.11
  630.3 4.2 fusion.110
  635.8 4.0 convolution_add_fusion.10
  639.8 4.0 fusion.111
  645.1 5.5 fusion.12
  650.6 2.3 reshape.307
  655.0 10.3 %conditional.9 = (f32[589824]{0:T(1024)S(1)}) conditional(s32[]{:T(128)} %convert_element_type.113, () %tuple.42, f32[2654208]{0:T(1024)} %all-gather.6.cloned.1.call-done), branch_computations={%region_33.34_spmd, %region_34.36_spmd} | conditional | flops 18360188928 | bytes 110887024 | solution.py:229
  668.1 2.6 fusion.65
  670.7 228.7 %all-reduce.10.cloned.1.call-done = f32[2654208]{0:T(1024)} async-done(((f32[2654208]{0:T(1024)}), f32[2654208]{0:T(1024)}) %all-reduce.10.cloned.1.call-update) | async-done | bytes 10616848
  899.5 3.7 dynamic-slice_subtract_fusion
  (215 shorter events, 73.5 us)
Async XLA Ops:
  7.2 3.1 copy-start.55
  7.2 47.2 %copy-start.58 = (s32[2]{0:T(128)S(1)}, s32[2]{0:T(128)}, u32[]{:S(2)}) copy-start(s32[2]{0:T(128)} %param.18) | copy-start | bytes 28
  7.2 47.8 %copy-start.3 = (bf16[2,256,384]{2,1,0:T(8,128)(2,1)S(1)}, bf16[2,256,384]{2,1,0:T(8,128)(2,1)}, u32[]{:S(2)}) copy-start(bf16[2,256,384]{2,1,0:T(8,128)(2,1)} %param.16) | copy-start | bytes 1179652
  7.2 68.0 %all-gather.4.cloned.1.call-start = ((), (), s32[]{:S(2)}) async-start(), calls=%async_computation | async-start | bytes 6635520 | tf_op jit(solution)/shard_map/all_gather | solution.py:210
  10.3 375.5 %all-reduce.8.cloned.1.call-start = ((), (), s32[]{:S(2)}) async-start(), calls=%async_computation.3 | async-start | bytes 21233664
  55.0 43.3 %copy-start.46 = (bf16[2,384]{1,0:T(2,128)(2,1)}, bf16[2,384]{1,0:T(2,128)(2,1)S(1)}, u32[]{:S(2)}) copy-start(bf16[2,384]{1,0:T(2,128)(2,1)S(1)} %gather_fusion) | copy-start | bytes 4612
  55.2 44.3 %copy-start.34 = (f32[2,256]{1,0:T(2,128)}, f32[2,256]{1,0:T(2,128)S(1)}, u32[]{:S(2)}) copy-start(f32[2,256]{1,0:T(2,128)S(1)} %broadcast_multiply_fusion.2) | copy-start | bytes 6148
  55.5 25.6 %copy-start.42 = (f32[2,256]{1,0:T(2,128)}, f32[2,256]{1,0:T(2,128)S(1)}, u32[]{:S(2)}) copy-start(f32[2,256]{1,0:T(2,128)S(1)} %fusion.69) | copy-start | bytes 6148
  55.5 42.8 %copy-start.52 = (pred[2]{0:T(512)(128)(4,1)}, pred[2]{0:T(512)(128)(4,1)S(1)}, u32[]{:S(2)}) copy-start(pred[2]{0:T(512)(128)(4,1)S(1)} %compare_and_fusion) | copy-start | bytes 10
  55.5 44.0 %copy-start.44 = (f32[2,256]{1,0:T(2,128)}, f32[2,256]{1,0:T(2,128)S(1)}, u32[]{:S(2)}) copy-start(f32[2,256]{1,0:T(2,128)S(1)} %fusion.85) | copy-start | bytes 6148
  90.3 2.2 slice-start
  98.2 3.3 copy-start.15
  99.5 3.5 copy-start.37
  99.5 3.5 copy-start.39
  101.6 1.5 copy-start.16
  105.5 2.9 copy-start.20
  105.5 1.4 copy-start.30
  107.0 1.5 copy-start.26
  107.0 1.5 copy-start.29
  111.2 2.2 copy-start.28
  115.5 2.5 copy-start.14
  115.5 2.5 copy-start.25
  115.5 2.4 copy-start.38
  118.0 4.2 copy-start.32
  127.1 2.5 copy-start.22
  144.6 3.4 copy-start.21
  146.9 1.6 copy-start.19
  148.0 3.6 copy-start.2
  153.1 3.5 copy-start.13
  156.6 1.5 copy-start.33
  156.6 1.5 copy-start.35
  156.6 1.5 copy-start.40
  156.6 1.5 copy-start.45
  158.1 2.5 copy-start.17
  161.4 1.4 copy-start.51
  161.4 1.4 copy-start.57
  161.4 1.4 copy-start.56
  161.4 1.4 copy-start.50
  161.4 2.0 copy-start.47
  167.0 4.1 copy-start.10
  171.1 2.7 copy-start.8
  173.8 2.5 copy-start.7
  178.0 280.6 %all-reduce.6.cloned.1.call-start = ((), (), s32[]{:S(2)}) async-start(), calls=%async_computation.1 | async-start | bytes 5308416 | tf_op jit(solution)/shard_map/psum | solution.py:215
  389.2 69.3 %copy-start.23 = (f32[663552]{0:T(1024)S(1)}, f32[663552]{0:T(1024)}, u32[]{:S(2)}) copy-start(f32[663552]{0:T(1024)} %param.20) | copy-start | bytes 7962628
  389.2 178.5 %all-gather.6.cloned.1.call-start = ((), (), s32[]{:S(2)}) async-start(), calls=%async_computation.2 | async-start | bytes 13271040 | tf_op jit(solution)/shard_map/all_gather | solution.py:217
  462.1 437.3 %all-reduce.10.cloned.1.call-start = ((), (), s32[]{:S(2)}) async-start(), calls=%async_computation.4 | async-start | bytes 21233664
  666.8 232.6 %copy-start.5 = (f32[663552]{0:T(1024)S(1)}, f32[663552]{0:T(1024)}, u32[]{:S(2)}) copy-start(f32[663552]{0:T(1024)} %param.19) | copy-start | bytes 7962628
  899.5 3.7 copy-start.6
  (15 other events, 14.5 us)
Sparse Core Ops, SparseCore 0:
  10.4 64.7 all-gather.3
  178.1 207.6 all-reduce.7
  389.3 69.1 all-reduce.5
  462.2 105.4 all-gather.5
  667.0 232.4 all-reduce.9
where the time goes:
time: 916 us; the launch traced here: 912 us
  waiting for transfers between devices  629 us (69%)
  matrix products  80.4 us (9%)
  local copies, waits for them, and re-layouts  77.9 us (9%)
  blocking collectives  44.1 us (5%)
  loops' own time  36.2 us (4%)
  other arithmetic  28.1 us (3%)
  between operations  15.4 us (2%)
    unnamed x7, waiting for transfers between devices  435 us
    all_gather x1, waiting for transfers between devices, on_device(): whole_mom = lax.all_gather(new_momentum, 'fsdp', axis=0, tiled=True)  106 us
    psum x1, waiting for transfers between devices, on_device(): full_grad = lax.psum(group_part, 'rep')  69.3 us
    all_gather x1, blocking collectives, on_device(): cond_table = lax.all_gather(conditions, ('fsdp', 'rep'), axis=0, tiled=True)  44.1 us
    another operation x5, loops' own time, on_device(): lax.cond(fsdp_rank == owner_rank, scaled_update, empty_update, piece, fac...  36.2 us
    unnamed x133, local copies, waits for them, and re-layouts  26.7 us
    dot_general x14, matrix products, matmul(): return jnp.dot(lhs_array, rhs_array, preferred_element_type=jnp.float32)  22 us
    slice x14, local copies, waits for them, and re-layouts, unpack(): flat_vec[offset:offset + rows_count * cols_count]  20.3 us
  transfers between devices with their start and end apart: 5, of which 5 were waited for; matrix products, arithmetic and copies ran while one was open for 0% of the time, Pallas kernels for 0%

commit v1 on v0

--- a/solution.py
+++ b/solution.py
@@ -212,7 +212,11 @@
     back_flat = lax.all_gather(low_params, "fsdp", axis=0, tiled=True)
     grad_tokens, flat_grads = backward_pass(kept_state, unpack(back_flat), cotangent)
     group_part = lax.psum_scatter(flat_grads, "fsdp", scatter_dimension=0, tiled=True)
-    full_grad = lax.psum(group_part, "rep")
+    full_grad = group_part
+    for hop in (1, 2, 4):
+        full_grad = full_grad + lax.ppermute(
+            full_grad, "rep", [(dev, dev ^ hop) for dev in range(8)]
+        )
     new_momentum = MOMENTUM_RATE * momentum + full_grad
     whole_mom = lax.all_gather(new_momentum, "fsdp", axis=0, tiled=True)
     fsdp_rank = lax.axis_index("fsdp")

time: 916 us -> 1030 us (1.12)
  waiting for transfers between devices: 629 us -> 738 us
    ppermute x0 -> x3, waiting for transfers between devices: none -> 177 us  [on_device(): lax.ppermute(full_grad, 'rep', [(dev, dev ^ hop) for dev in range(8)])]
    psum x1 -> x0, waiting for transfers between devices: 69.3 us -> none  [on_device(): full_grad = lax.psum(group_part, 'rep')]
    unnamed x133 -> x130, local copies, waits for them, and re-layouts: 26.7 us -> 23.5 us
    unnamed x7 -> x6, waiting for transfers between devices: 435 us -> 435 us
  transfers between devices with their start and end apart: 5 -> 7, of which waited for: 5 -> 7; matrix products, arithmetic and copies ran while one was open for 0% -> 0% of each run, Pallas kernels for 0% -> 0%
where the time goes in v1:
time: 1030 us; the launch traced here: 1020 us
  waiting for transfers between devices  738 us (72%)
  matrix products  80.4 us (8%)
  local copies, waits for them, and re-layouts  74.7 us (7%)
  blocking collectives  44.1 us (4%)
  loops' own time  36.1 us (4%)
  other arithmetic  29.5 us (3%)
  between operations  15.4 us (1%)
    unnamed x6, waiting for transfers between devices  435 us
    ppermute x3, waiting for transfers between devices, on_device(): lax.ppermute(full_grad, 'rep', [(dev, dev ^ hop) for dev in range(8)])  177 us
    all_gather x1, waiting for transfers between devices, on_device(): whole_mom = lax.all_gather(new_momentum, 'fsdp', axis=0, tiled=True)  106 us
    all_gather x1, blocking collectives, on_device(): cond_table = lax.all_gather(conditions, ('fsdp', 'rep'), axis=0, tiled=True)  44.1 us
    another operation x5, loops' own time, on_device(): lax.cond(fsdp_rank == owner_rank, scaled_update, empty_update, piece, fac...  36.1 us
    unnamed x130, local copies, waits for them, and re-layouts  23.5 us
    dot_general x14, matrix products, matmul(): return jnp.dot(lhs_array, rhs_array, preferred_element_type=jnp.float32)  22.1 us
  transfers between devices with their start and end apart: 7, of which 7 were waited for; matrix products, arithmetic and copies ran while one was open for 0% of the time, Pallas kernels for 0%

profile of v1, /device:TPU:0, one launch (start us, length us, event | category | flops | bytes accessed | tf_op | source)
XLA Modules:
  0.0 1022.4 jit_solution(5635797342942901850)
XLA Ops:
  7.2 3.0 convert_element_type.90
  10.3 44.1 %all-gather = bf16[32,2,384]{2,1,0:T(2,128)(2,1)S(1)} all-gather(bf16[1,2,384]{2,1,0:T(2,128)(2,1)S(1)} %bitcast.245), channel_id=1, replica_groups=mesh['fsdp'=4,'rep'=8] {'fsdp','rep'}, dimensions={0}, use_global_device_ids=true | all-gather | bytes 50688 | tf_op jit(solution)/shard_map/all_gather | solution.py:207
  55.5 19.7 %all-gather.4.cloned.1.call-done = bf16[2654208]{0:T(1024)(128)(2,1)} async-done(((bf16[663552]{0:T(1024)(128)(2,1)}), bf16[2654208]{0:T(1024)(128)(2,1)}) %all-gather.4.cloned.1.call-update) | async-done | bytes 5308432 | tf_op jit(solution)/shard_map/all_gather | solution.py:210
  81.1 2.0 slice.162
  88.2 2.1 reshape.357
  90.4 2.2 slice.172
  92.5 3.0 slice.157
  95.5 2.8 copy.42
  99.5 2.1 fusion.67
  108.5 2.8 fusion.36
  111.2 2.2 fusion.116
  115.6 2.4 fusion.117
  118.0 2.5 fusion.72
  127.1 2.5 convolution_bitcast_fusion
  129.6 3.2 fusion.73
  132.9 5.2 fusion.49
  138.1 5.1 fusion.52
  144.6 2.2 copy.55
  153.1 3.4 reshape.341
  158.1 2.5 fusion.68
  164.9 2.1 reshape.337
  167.0 4.1 constant_dynamic-update-slice_fusion.6
  179.8 206.0 %all-reduce.5.cloned.1.call-done = f32[2654208]{0:T(1024)} async-done(((f32[2654208]{0:T(1024)}), f32[2654208]{0:T(1024)}) %all-reduce.5.cloned.1.call-update) | async-done | bytes 10616848
  387.8 4.9 collective-permute-done
  396.3 58.1 %collective-permute-done.1 = f32[663552]{0:T(1024)S(1)} collective-permute-done((f32[663552]{0:T(1024)S(1)}, f32[663552]{0:T(1024)S(1)}, u32[]{:S(2)}, u32[]{:S(2)}) %collective-permute-start.1) | collective-permute-done | bytes 2654240 | tf_op jit(solution)/shard_map/ppermute | solution.py:217
  454.7 2.5 collective-permute-start.2
  457.2 114.1 %collective-permute-done.2 = f32[663552]{0:T(1024)S(1)} collective-permute-done((f32[663552]{0:T(1024)S(1)}, f32[663552]{0:T(1024)S(1)}, u32[]{:S(2)}, u32[]{:S(2)}) %collective-permute-start.2) | collective-permute-done | bytes 2654240 | tf_op jit(solution)/shard_map/ppermute | solution.py:217
  571.3 2.8 multiply_add_fusion.3
  574.2 106.1 %all-gather.6.cloned.1.call-done = f32[2654208]{0:T(1024)} async-done(((f32[663552]{0:T(1024)}), f32[2654208]{0:T(1024)}) %all-gather.6.cloned.1.call-update) | async-done | bytes 10616848 | tf_op jit(solution)/shard_map/all_gather | solution.py:221
  680.3 9.3 conditional.5
  689.6 2.1 constant_dynamic-update-slice_fusion.7
  691.7 14.8 %conditional.6 = (f32[442368]{0:T(1024)S(1)}) conditional(s32[]{:T(128)} %convert_element_type.111, () %tuple.39, f32[2654208]{0:T(1024)} %all-gather.6.cloned.1.call-done), branch_computations={%region_23.24_spmd, %region_24.26_spmd} | conditional | flops 14274772992 | bytes 35389476 | solution.py:233
  707.8 15.7 %conditional.7 = (f32[147456]{0:T(1024)S(1)}) conditional(s32[]{:T(128)} %convert_element_type.112, () %tuple.40, f32[2654208]{0:T(1024)} %all-gather.6.cloned.1.call-done), branch_computations={%region_26.27_spmd, %region_27.29_spmd} | conditional | flops 6118096896 | bytes 16515108 | solution.py:233
  724.4 41.5 %conditional.8 = (f32[589824]{0:T(1024)S(1)}) conditional(s32[]{:T(128)} %convert_element_type.112, () %tuple.41, f32[2654208]{0:T(1024)} %all-gather.6.cloned.1.call-done), branch_computations={%region_29.30_spmd, %region_30.32_spmd} | conditional | flops 18353111040 | bytes 44826660 | solution.py:233
  724.4 2.9 multiply_reduce_fusion.3
  728.0 3.2 slice_divide_fusion.3
  731.2 2.4 div.75
  733.7 4.0 fusion.109
  738.9 4.0 convolution_add_fusion.11
  742.9 4.2 fusion.110
  748.4 4.0 convolution_add_fusion.10
  752.4 4.0 fusion.111
  757.7 5.5 fusion.12
  763.2 2.3 reshape.307
  767.5 10.2 conditional.9
  780.6 2.6 fusion.65
  783.2 228.9 %all-reduce.7.cloned.1.call-done = f32[2654208]{0:T(1024)} async-done(((f32[2654208]{0:T(1024)}), f32[2654208]{0:T(1024)}) %all-reduce.7.cloned.1.call-update) | async-done | bytes 10616848
  1012.1 3.5 dynamic-slice_subtract_fusion
  (217 shorter events, 81.5 us)
Async XLA Ops:
  7.2 3.1 copy-start.54
  7.2 47.2 %copy-start.57 = (s32[2]{0:T(128)S(1)}, s32[2]{0:T(128)}, u32[]{:S(2)}) copy-start(s32[2]{0:T(128)} %param.18) | copy-start | bytes 28
  7.2 47.8 %copy-start.3 = (bf16[2,256,384]{2,1,0:T(8,128)(2,1)S(1)}, bf16[2,256,384]{2,1,0:T(8,128)(2,1)}, u32[]{:S(2)}) copy-start(bf16[2,256,384]{2,1,0:T(8,128)(2,1)} %param.16) | copy-start | bytes 1179652
  7.2 68.0 %all-gather.4.cloned.1.call-start = ((), (), s32[]{:S(2)}) async-start(), calls=%async_computation | async-start | bytes 6635520 | tf_op jit(solution)/shard_map/all_gather | solution.py:210
  10.3 375.5 %all-reduce.5.cloned.1.call-start = ((), (), s32[]{:S(2)}) async-start(), calls=%async_computation.2 | async-start | bytes 21233664
  55.0 43.3 %copy-start.45 = (bf16[2,384]{1,0:T(2,128)(2,1)}, bf16[2,384]{1,0:T(2,128)(2,1)S(1)}, u32[]{:S(2)}) copy-start(bf16[2,384]{1,0:T(2,128)(2,1)S(1)} %gather_fusion) | copy-start | bytes 4612
  55.2 44.3 %copy-start.33 = (f32[2,256]{1,0:T(2,128)}, f32[2,256]{1,0:T(2,128)S(1)}, u32[]{:S(2)}) copy-start(f32[2,256]{1,0:T(2,128)S(1)} %broadcast_multiply_fusion.2) | copy-start | bytes 6148
  55.5 25.7 %copy-start.41 = (f32[2,256]{1,0:T(2,128)}, f32[2,256]{1,0:T(2,128)S(1)}, u32[]{:S(2)}) copy-start(f32[2,256]{1,0:T(2,128)S(1)} %fusion.69) | copy-start | bytes 6148
  55.5 42.8 %copy-start.51 = (pred[2]{0:T(512)(128)(4,1)}, pred[2]{0:T(512)(128)(4,1)S(1)}, u32[]{:S(2)}) copy-start(pred[2]{0:T(512)(128)(4,1)S(1)} %compare_and_fusion) | copy-start | bytes 10
  55.5 44.0 %copy-start.43 = (f32[2,256]{1,0:T(2,128)}, f32[2,256]{1,0:T(2,128)S(1)}, u32[]{:S(2)}) copy-start(f32[2,256]{1,0:T(2,128)S(1)} %fusion.85) | copy-start | bytes 6148
  90.4 2.2 slice-start
  98.3 3.3 copy-start.14
  99.5 3.5 copy-start.36
  99.5 3.5 copy-start.38
  101.6 1.5 copy-start.15
  105.5 2.9 copy-start.19
  105.5 1.4 copy-start.29
  107.0 1.5 copy-start.25
  107.0 1.5 copy-start.28
  111.2 2.2 copy-start.27
  115.5 2.5 copy-start.13
  115.5 2.5 copy-start.24
  115.6 2.4 copy-start.37
  118.0 4.2 copy-start.31
  127.1 2.5 copy-start.21
  144.6 3.4 copy-start.20
  146.8 1.6 copy-start.18
  147.9 3.6 copy-start.2
  153.1 3.5 copy-start.12
  156.5 1.5 copy-start.32
  156.5 1.5 copy-start.34
  156.5 1.5 copy-start.39
  156.6 1.5 copy-start.44
  158.0 2.6 copy-start.16
  161.4 1.4 copy-start.56
  161.4 1.4 copy-start.55
  161.4 1.4 copy-start.49
  161.4 2.0 copy-start.46
  167.0 4.1 copy-start.9
  171.1 2.7 copy-start.7
  173.8 2.5 copy-start.6
  177.9 502.3 %all-gather.6.cloned.1.call-start = ((), (), s32[]{:S(2)}) async-start(), calls=%async_computation.1 | async-start | bytes 13271040 | tf_op jit(solution)/shard_map/all_gather | solution.py:221
  387.7 5.0 collective-permute-start
  394.7 176.6 %copy-start.22 = (f32[663552]{0:T(1024)S(1)}, f32[663552]{0:T(1024)}, u32[]{:S(2)}) copy-start(f32[663552]{0:T(1024)} %param.20) | copy-start | bytes 7962628
  394.8 59.7 %collective-permute-start.1 = (f32[663552]{0:T(1024)S(1)}, f32[663552]{0:T(1024)S(1)}, u32[]{:S(2)}, u32[]{:S(2)}) collective-permute-start(f32[663552]{0:T(1024)S(1)} %dynamic-slice_add_fusion), channel_id=1, source_target_pairs={{0,2},{1,3},{2,0},{3,1},{4,6},{5,7},{6,4},{7,5},{8,10},{9,11},{10,... | collective-permute-start | bytes 7962632 | tf_op jit(solution)/shard_map/ppermute | solution.py:217
  454.7 116.6 %collective-permute-start.2 = (f32[663552]{0:T(1024)S(1)}, f32[663552]{0:T(1024)S(1)}, u32[]{:S(2)}, u32[]{:S(2)}) collective-permute-start(f32[663552]{0:T(1024)S(1)} %add.253), channel_id=1, source_target_pairs={{0,4},{1,5},{2,6},{3,7},{4,0},{5,1},{6,2},{7,3},{8,12},{9,13},{10,... | collective-permute-start | bytes 7962632 | tf_op jit(solution)/shard_map/ppermute | solution.py:217
  574.1 438.0 %all-reduce.7.cloned.1.call-start = ((), (), s32[]{:S(2)}) async-start(), calls=%async_computation.3 | async-start | bytes 21233664
  779.3 232.8 %copy-start.5 = (f32[663552]{0:T(1024)S(1)}, f32[663552]{0:T(1024)}, u32[]{:S(2)}) copy-start(f32[663552]{0:T(1024)} %param.19) | copy-start | bytes 7962628
  (16 other events, 15.9 us)
Sparse Core Ops, SparseCore 0:
  10.4 64.7 all-gather.3
  178.1 207.6 all-reduce.4
  574.3 105.9 all-gather.5
  779.4 232.6 all-reduce.6
